TPU v7x, 512 devices: a whole 4x4x16 slice. The times are simulated.
512 devices in a mesh: dp: 16 (over x_hi, y, core), tensor: 32 (over z, x_lo).
Axes of the slice: x: 4 (x_hi: 2, x_lo: 2; x = x_hi * 2 + x_lo), y: 4, z: 16, core: 2. Of those that a mesh axis runs over, the one named last changes fastest.
Arguments:
- features: bfloat16 [8192, 16384], P('tensor', 'dp'), may hold values from -6 to 6
- up_blocks: bfloat16 [64, 128, 512], P('tensor', 'dp'), may hold values from -0.5 to 0.5
- down_blocks: bfloat16 [64, 512, 128], P('tensor', 'dp'), may hold values from -0.25 to 0.25
- out_cotangent: bfloat16 [8192, 16384], P('tensor', 'dp'), may hold values from -6 to 6
Outputs:
- mixed: bfloat16 [8192, 16384], P('tensor', 'dp')
- feature_grad: bfloat16 [8192, 16384], P('tensor', 'dp')
- up_grad: float32 [64, 128, 512], P('tensor', 'dp')
- down_grad: float32 [64, 512, 128], P('tensor', 'dp')
All inputs are finite; a program needn't handle non-finite values.
Results may differ from a plain program's by a relative error of at most 0.023.
Values may be sent and summed in bfloat16 or wider, within the bound.
No kernel may reach another device: no remote copies, remote signals or barrier semaphores. Data moves between devices by JAX's collectives and lax.ppermute only.
A program may use at most 64 MiB of HBM per device.

v0:
```python
import jax
import jax.numpy as jnp
from jax import lax
from jax.sharding import PartitionSpec as P

NB = 64
BIN = 128
BOUT = 512
J_UP = 8
J_DN = 2


def gelu_value(v):
    return 0.5 * v * (1.0 + lax.erf(v * 0.7071067811865476))


def gelu_slope(v):
    return (
        0.5 * (1.0 + lax.erf(v * 0.7071067811865476))
        + v * jnp.exp(-0.5 * v * v) * 0.3989422804014327
    )


def per_device(features, up_blocks, down_blocks, out_cotangent):
    local_blocks = up_blocks.shape[0]
    tok_local = features.shape[1]
    dp_count = lax.axis_size("dp")
    x_local = features.reshape(local_blocks, BIN, tok_local)
    down_whole = lax.all_gather(down_blocks, "dp", axis=1, tiled=True)
    down_four = down_whole.reshape(local_blocks, BOUT, NB, J_DN)
    piece = lax.all_gather(up_blocks, "dp", axis=1, tiled=True)
    rows_now = piece.shape[1]
    x_rows = x_local
    pre_sum = jnp.einsum(
        "bkgj,bkt->gbjt",
        piece.reshape(local_blocks, rows_now, NB, J_UP),
        x_rows,
        preferred_element_type=jnp.float32,
    )
    pre = pre_sum.astype(jnp.bfloat16)
    received = lax.all_to_all(pre, "tensor", split_axis=0, concat_axis=1, tiled=True)
    items = received.shape[3]
    permuted = received.reshape(local_blocks, BOUT, items)
    hidden_act = gelu_value(permuted.astype(jnp.float32)).astype(jnp.bfloat16)
    blockout = jnp.einsum(
        "gmt,gmbj->bgjt", hidden_act, down_four, preferred_element_type=jnp.float32
    ).astype(jnp.bfloat16)
    returned = lax.all_to_all(blockout, "tensor", split_axis=0, concat_axis=1, tiled=True)
    permuted, act, mixed_blocks = (permuted, hidden_act, returned.reshape(local_blocks, BIN, items))
    mixed = mixed_blocks.reshape(local_blocks * BIN, tok_local)
    shaped = out_cotangent.reshape(local_blocks, NB, J_DN, tok_local)
    dblock = lax.all_to_all(shaped, "tensor", split_axis=1, concat_axis=0, tiled=True)
    dact = jnp.einsum("gmbj,bgjt->gmt", down_four, dblock, preferred_element_type=jnp.float32)
    dperm = (dact * gelu_slope(permuted.astype(jnp.float32))).astype(jnp.bfloat16)
    term = jnp.einsum("gmt,bgjt->mgbj", act, dblock, preferred_element_type=jnp.float32)
    down_share = lax.psum_scatter(
        term.reshape(BOUT // dp_count * lax.axis_size("dp"), local_blocks, BIN).astype(
            jnp.bfloat16
        ),
        "dp",
        scatter_dimension=0,
        tiled=True,
    ).astype(jnp.float32)
    down_grad = down_share.transpose(1, 0, 2)
    dpre = lax.all_to_all(
        dperm.reshape(local_blocks, NB, J_UP, tok_local),
        "tensor",
        split_axis=1,
        concat_axis=0,
        tiled=True,
    )
    x_rows = x_local
    term = jnp.einsum("bkt,gbjt->kbgj", x_rows, dpre, preferred_element_type=jnp.float32)
    up_share = lax.psum_scatter(
        term.reshape(BIN // dp_count * lax.axis_size("dp"), local_blocks, BOUT).astype(
            jnp.bfloat16
        ),
        "dp",
        scatter_dimension=0,
        tiled=True,
    ).astype(jnp.float32)
    up_grad = up_share.transpose(1, 0, 2)
    piece = lax.all_gather(up_blocks, "dp", axis=1, tiled=True)
    rows_now = piece.shape[1]
    fgrad = jnp.einsum(
        "bkgj,gbjt->bkt",
        piece.reshape(local_blocks, rows_now, NB, J_UP),
        dpre,
        preferred_element_type=jnp.float32,
    ).astype(jnp.bfloat16)
    feature_grad = fgrad.reshape(local_blocks * BIN, tok_local)
    return (mixed, feature_grad, up_grad, down_grad)


def solution(mesh):
    placed = (
        P("tensor", "dp"),
        P("tensor", "dp", None),
        P("tensor", "dp", None),
        P("tensor", "dp"),
    )
    return jax.shard_map(
        per_device,
        mesh=mesh,
        in_specs=placed,
        out_specs=(
            P("tensor", "dp"),
            P("tensor", "dp"),
            P("tensor", "dp", None),
            P("tensor", "dp", None),
        ),
        check_vma=False,
    )
```

profile of v0, /device:TPU:32, one launch (start us, length us, event | category | flops | bytes accessed | tf_op | source)
XLA Modules:
  0.0 538.5 jit_solution(7308746396229365794)
XLA Ops:
  7.2 0.0 copy-start
  7.2 1.3 reshape.41
  8.5 1.2 copy.54
  9.6 16.3 %all-to-all-start.2 = ((bf16[2,64,2,1024]{3,2,0,1:T(2,128)(2,1)}), bf16[2,64,2,1024]{3,2,0,1:T(2,128)(2,1)S(1)}, u32[]{:S(2)}, u32[]{:S(2)}) async-start(bf16[2,64,2,1024]{3,2,0,1:T(2,128)(2,1)} %copy.54), calls=%async_computation.2 | async-start | bytes 1048576 | tf_op jit(solution)/shard_map/all_to_all | solution.py:52
  25.9 0.7 copy.45
  26.7 25.2 %all_gather.7 = bf16[2,128,512]{2,0,1:T(2,128)(2,1)S(1)} all-gather(bf16[2,8,512]{2,0,1:T(2,128)(2,1)S(1)} %copy.45), channel_id=1, replica_groups=mesh['dp'=16,'tensor'=32] {'dp'}, dimensions={1}, use_global_device_ids=true | all-gather | bytes 278528 | tf_op jit(solution)/shard_map/all_gather | solution.py:31
  51.9 0.2 copy.46
  52.1 0.7 convert_bitcast_fusion
  52.8 0.0 copy-start.4
  52.8 2.5 copy.48
  55.3 2.0 all-to-all-done.2
  57.4 10.2 %all-to-all-start = ((bf16[64,2,8,1024]{3,2,1,0:T(8,128)(2,1)}), bf16[64,2,8,1024]{3,2,1,0:T(8,128)(2,1)S(1)}, u32[]{:S(2)}, u32[]{:S(2)}) async-start(bf16[64,2,8,1024]{3,2,1,0:T(8,128)(2,1)} %copy.48), calls=%async_computation | async-start | bytes 4194304 | tf_op jit(solution)/shard_map/all_to_all | solution.py:41
  67.6 22.2 %all_gather.8 = bf16[2,512,128]{2,1,0:T(8,128)(2,1)} all-gather(bf16[2,32,128]{2,1,0:T(8,128)(2,1)S(1)} %copy-done.4), channel_id=1, replica_groups=mesh['dp'=16,'tensor'=32] {'dp'}, dimensions={1}, use_global_device_ids=true | all-gather | bytes 278528 | tf_op jit(solution)/shard_map/all_gather | solution.py:29
  89.8 1.8 copy.50
  91.7 1.2 copy.56
  92.9 1.2 all_to_all.51
  94.1 0.0 copy-start.1
  94.1 73.4 %all-to-all-done = bf16[64,2,8,1024]{3,2,1,0:T(8,128)(2,1)S(1)} async-done(((bf16[64,2,8,1024]{3,2,1,0:T(8,128)(2,1)}), bf16[64,2,8,1024]{3,2,1,0:T(8,128)(2,1)S(1)}, u32[]{:S(2)}, u32[]{:S(2)}) %all-to-all-start) | async-done | bytes 2097184 | tf_op jit(solution)/shard_map/all_to_all | solution.py:41
  167.5 0.5 copy.49
  168.0 1.2 fusion.7
  169.2 1.5 fusion.14
  170.7 1.6 copy.58
  172.3 4.6 all-to-all-start.3
  176.8 0.5 fusion.19
  177.3 1.3 copy.52
  178.6 97.2 %all-to-all-done.3 = bf16[2,64,8,1024]{3,2,0,1:T(8,128)(2,1)} async-done(((bf16[2,64,8,1024]{3,2,0,1:T(8,128)(2,1)}), bf16[2,64,8,1024]{3,2,0,1:T(8,128)(2,1)}, u32[]{:S(2)}, u32[]{:S(2)}) %all-to-all-start.3) | async-done | bytes 2097184 | tf_op jit(solution)/shard_map/all_to_all | solution.py:65
  275.8 4.4 all-to-all-start.1
  280.2 0.0 all-reduce.3.cloned.1.call-start
  280.3 1.3 dynamic-slice
  282.2 1.9 fusion.26
  284.1 0.3 copy.63
  284.3 1.0 copy.64
  285.4 0.0 all-reduce.3.cloned.1.call-update
  285.4 0.2 reduce-scatter.4.cloned.1.call-start
  285.6 5.1 copy.84
  290.7 2.7 all_to_all.55
  293.5 0.7 fusion.25
  294.2 0.9 copy.61
  295.1 1.8 copy.74
  296.9 0.0 reduce-scatter.4.cloned.1.call-update
  296.9 138.8 %all-reduce.3.cloned.1.call-done = bf16[512,2,128]{2,1,0:T(2,128)(2,1)} async-done(((bf16[512,2,128]{2,1,0:T(2,128)(2,1)}), bf16[512,2,128]{2,1,0:T(2,128)(2,1)}) %all-reduce.3.cloned.1.call-update) | async-done | bytes 262160
  435.7 0.7 convert_bitcast_fusion.1
  436.5 0.6 copy.65
  437.1 1.2 copy.53
  438.2 2.0 reshape_reshape.3
  440.3 1.3 fusion.15
  441.6 88.8 %reduce-scatter.4.cloned.1.call-done = bf16[8,1024]{1,0:T(8,128)(2,1)} async-done(((bf16[128,1024]{1,0:T(8,128)(2,1)}), bf16[8,1024]{1,0:T(8,128)(2,1)}) %reduce-scatter.4.cloned.1.call-update) | async-done | bytes 16400
  530.4 1.3 convert_bitcast_fusion.2
  (8 shorter events, 0.0 us)
Async XLA Ops:
  7.2 44.9 %copy-start = (bf16[256,1024]{1,0:T(8,128)(2,1)S(1)}, bf16[256,1024]{1,0:T(8,128)(2,1)}, u32[]{:S(2)}) copy-start(bf16[256,1024]{1,0:T(8,128)(2,1)} %param.4) | copy-start | bytes 1572868
  9.6 47.7 %all-to-all-start.2 = ((bf16[2,64,2,1024]{3,2,0,1:T(2,128)(2,1)}), bf16[2,64,2,1024]{3,2,0,1:T(2,128)(2,1)S(1)}, u32[]{:S(2)}, u32[]{:S(2)}) async-start(bf16[2,64,2,1024]{3,2,0,1:T(2,128)(2,1)} %copy.54), calls=%async_computation.2 | async-start | bytes 1048576 | tf_op jit(solution)/shard_map/all_to_all | solution.py:52
  52.8 14.8 %copy-start.4 = (bf16[2,32,128]{2,1,0:T(8,128)(2,1)S(1)}, bf16[2,32,128]{2,1,0:T(8,128)(2,1)}, u32[]{:S(2)}) copy-start(bf16[2,32,128]{2,1,0:T(8,128)(2,1)} %param.6) | copy-start | bytes 49156
  57.4 110.1 %all-to-all-start = ((bf16[64,2,8,1024]{3,2,1,0:T(8,128)(2,1)}), bf16[64,2,8,1024]{3,2,1,0:T(8,128)(2,1)S(1)}, u32[]{:S(2)}, u32[]{:S(2)}) async-start(bf16[64,2,8,1024]{3,2,1,0:T(8,128)(2,1)} %copy.48), calls=%async_computation | async-start | bytes 4194304 | tf_op jit(solution)/shard_map/all_to_all | solution.py:41
  94.1 75.0 %copy-start.1 = (bf16[64,2,2,1024]{3,0,2,1:T(8,128)(2,1)}, bf16[64,2,2,1024]{3,0,2,1:T(8,128)(2,1)S(1)}, u32[]{:S(2)}) copy-start(bf16[64,2,2,1024]{3,0,2,1:T(8,128)(2,1)S(1)} %all_to_all.51) | copy-start | bytes 1572868
  168.0 1.2 copy-start.2
  170.7 6.1 %copy-start.3 = (bf16[2,512,128]{1,0,2:T(2,128)(2,1)S(1)}, bf16[2,512,128]{1,0,2:T(2,128)(2,1)}, u32[]{:S(2)}) copy-start(bf16[2,512,128]{1,0,2:T(2,128)(2,1)} %copy.50) | copy-start | bytes 786436
  172.3 103.5 %all-to-all-start.3 = ((bf16[2,64,8,1024]{3,2,0,1:T(8,128)(2,1)}), bf16[2,64,8,1024]{3,2,0,1:T(8,128)(2,1)}, u32[]{:S(2)}, u32[]{:S(2)}) async-start(bf16[2,64,8,1024]{3,2,0,1:T(8,128)(2,1)} %copy.58), calls=%async_computation.3 | async-start | bytes 4194304 | tf_op jit(solution)/shard_map/all_to_all | solution.py:65
  275.8 161.3 %all-to-all-start.1 = ((bf16[64,2,2,1024]{3,2,1,0:T(2,128)(2,1)}), bf16[64,2,2,1024]{3,2,1,0:T(2,128)(2,1)S(1)}, u32[]{:S(2)}, u32[]{:S(2)}) async-start(bf16[64,2,2,1024]{3,2,1,0:T(2,128)(2,1)} %copy.52), calls=%async_computation.1 | async-start | bytes 1048576 | tf_op jit(solution)/shard_map/all_to_all | solution.py:48
  280.2 155.5 %all-reduce.3.cloned.1.call-start = ((), (), s32[]{:S(2)}) async-start(), calls=%async_computation.6 | async-start | bytes 524288
  285.4 244.9 %reduce-scatter.4.cloned.1.call-start = ((), (), s32[]{:S(2)}) async-start(), calls=%async_computation.5 | async-start | bytes 278528
Sparse Core Ops, SparseCore 0:
  285.5 150.1 all-reduce.2
  440.9 89.3 reduce-scatter.3
where the time goes:
time: 539 us
  waiting for transfers between devices  400 us (74%)
  blocking collectives  47.4 us (9%)
  starting transfers between devices  35.7 us (7%)
  local copies, waits for them, and re-layouts  30.5 us (6%)
  between operations  14.9 us (3%)
  matrix products  6.54 us (1%)
    unnamed x4, waiting for transfers between devices  228 us
    all_to_all x1, waiting for transfers between devices, per_device(): lax.all_to_all(dperm.reshape(local_blocks, NB, J_UP, tok_local), 'tensor'...  97.2 us
    all_to_all x1, waiting for transfers between devices, per_device(): lax.all_to_all(pre, 'tensor', split_axis=0, concat_axis=1, tiled=True)  73.4 us
    all_gather x1, blocking collectives, per_device(): piece = lax.all_gather(up_blocks, 'dp', axis=1, tiled=True)  25.2 us
    all_gather x1, blocking collectives, per_device(): down_whole = lax.all_gather(down_blocks, 'dp', axis=1, tiled=True)  22.2 us
    all_to_all x1, starting transfers between devices, per_device(): lax.all_to_all(shaped, 'tensor', split_axis=1, concat_axis=0, tiled=True)  16.3 us
  transfers between devices with their start and end apart: 6, of which 5 were waited for; matrix products, arithmetic and copies ran while one was open for 5% of the time, Pallas kernels for 0%

commit v1 on v0

--- a/solution.py
+++ b/solution.py
@@ -8,6 +8,11 @@
 BOUT = 512
 J_UP = 8
 J_DN = 2
+
+
+def gather_over(block, mesh_axis, dim):
+    sent = jnp.stack([block] * lax.axis_size(mesh_axis))
+    return jnp.concatenate(lax.all_to_all(sent, mesh_axis, 0, 0), axis=dim)
 
 
 def gelu_value(v):
@@ -28,7 +33,7 @@
     x_local = features.reshape(local_blocks, BIN, tok_local)
     down_whole = lax.all_gather(down_blocks, "dp", axis=1, tiled=True)
     down_four = down_whole.reshape(local_blocks, BOUT, NB, J_DN)
-    piece = lax.all_gather(up_blocks, "dp", axis=1, tiled=True)
+    piece = gather_over(up_blocks, "dp", 1)
     rows_now = piece.shape[1]
     x_rows = x_local
     pre_sum = jnp.einsum(

time: 539 us -> 573 us (1.063)
  waiting for transfers between devices: 400 us -> 419 us
  local copies, waits for them, and re-layouts: 30.5 us -> 41.5 us
    another operation x0 -> x3, local copies, waits for them, and re-layouts: none -> 13.7 us  [the longest x2 12.2 us: per_device(): piece.reshape(local_blocks, rows_now, NB, J_UP)]
    all_to_all x1, waiting for transfers between devices: 2.03 us -> 15.6 us  [per_device(): lax.all_to_all(shaped, 'tensor', split_axis=1, concat_axis=0, tiled=True)]
    all_to_all x0 -> x1, waiting for transfers between devices: none -> 7.15 us  [gather_over(): return jnp.concatenate(lax.all_to_all(sent, mesh_axis, 0, 0), axis=dim)]
    all_to_all x0 -> x1, starting transfers between devices: none -> 7.03 us  [gather_over(): return jnp.concatenate(lax.all_to_all(sent, mesh_axis, 0, 0), axis=dim)]
  transfers between devices with their start and end apart: 6 -> 7, of which waited for: 5 -> 6; matrix products, arithmetic and copies ran while one was open for 5% -> 7% of each run, Pallas kernels for 0% -> 0%
where the time goes in v1:
time: 573 us; the launch traced here: 572 us
  waiting for transfers between devices  419 us (73%)
  blocking collectives  45.9 us (8%)
  local copies, waits for them, and re-layouts  41.5 us (7%)
  starting transfers between devices  39.1 us (7%)
  between operations  14.9 us (3%)
  matrix products  7.49 us (1%)
    unnamed x4, waiting for transfers between devices  229 us
    all_to_all x1, waiting for transfers between devices, per_device(): lax.all_to_all(dperm.reshape(local_blocks, NB, J_UP, tok_local), 'tensor'...  96.1 us
    all_to_all x1, waiting for transfers between devices, per_device(): lax.all_to_all(pre, 'tensor', split_axis=0, concat_axis=1, tiled=True)  71 us
    all_gather x1, blocking collectives, per_device(): down_whole = lax.all_gather(down_blocks, 'dp', axis=1, tiled=True)  23 us
    all_gather x1, blocking collectives, per_device(): piece = lax.all_gather(up_blocks, 'dp', axis=1, tiled=True)  22.9 us
    all_to_all x1, waiting for transfers between devices, per_device(): lax.all_to_all(shaped, 'tensor', split_axis=1, concat_axis=0, tiled=True)  15.6 us
    all_to_all x1, starting transfers between devices, per_device(): lax.all_to_all(shaped, 'tensor', split_axis=1, concat_axis=0, tiled=True)  15.4 us
    another operation x2, local copies, waits for them, and re-layouts, per_device(): piece.reshape(local_blocks, rows_now, NB, J_UP)  12.2 us
  transfers between devices with their start and end apart: 7, of which 6 were waited for; matrix products, arithmetic and copies ran while one was open for 7% of the time, Pallas kernels for 0%

profile of v1, /device:TPU:32, one launch (start us, length us, event | category | flops | bytes accessed | tf_op | source)
XLA Modules:
  0.0 571.5 jit_solution(15946319433359765933)
XLA Ops:
  7.2 1.5 stack.2
  8.7 7.0 %all-to-all-start = ((bf16[16,2,8,512]{3,2,1,0:T(8,128)(2,1)}), bf16[16,2,8,512]{3,2,1,0:T(8,128)(2,1)S(1)}, u32[]{:S(2)}, u32[]{:S(2)}) async-start(bf16[16,2,8,512]{3,2,1,0:T(8,128)(2,1)} %stack.2), calls=%async_computation | async-start | bytes 524288 | tf_op jit(solution)/shard_map/all_to_all | solution.py:15
  15.7 1.2 reshape.45
  17.0 1.2 copy.54
  18.1 7.2 %all-to-all-done = bf16[16,2,8,512]{3,2,1,0:T(8,128)(2,1)S(1)} async-done(((bf16[16,2,8,512]{3,2,1,0:T(8,128)(2,1)}), bf16[16,2,8,512]{3,2,1,0:T(8,128)(2,1)S(1)}, u32[]{:S(2)}, u32[]{:S(2)}) %all-to-all-start) | async-done | bytes 262176 | tf_op jit(solution)/shard_map/all_to_all | solution.py:15
  25.3 15.4 %all-to-all-start.3 = ((bf16[2,64,2,1024]{3,2,0,1:T(2,128)(2,1)}), bf16[2,64,2,1024]{3,2,0,1:T(2,128)(2,1)S(1)}, u32[]{:S(2)}, u32[]{:S(2)}) async-start(bf16[2,64,2,1024]{3,2,0,1:T(2,128)(2,1)} %copy.54), calls=%async_computation.3 | async-start | bytes 1048576 | tf_op jit(solution)/shard_map/all_to_all | solution.py:57
  40.7 5.9 %reshape_reshape.6 = bf16[2,128,64,8]{3,2,1,0:T(8,128)(2,1)} reshape(bf16[2,16,8,512]{3,2,1,0:T(8,128)(2,1)S(1)} %copy.46) | data formatting | bytes 524288 | tf_op jit(solution)/shard_map/reshape;reshape | solution.py:41
  46.6 6.3 %copy.47 = bf16[2,128,64,8]{1,2,3,0:T(8,128)(2,1)S(1)} copy(bf16[2,128,64,8]{3,2,1,0:T(8,128)(2,1)} %reshape_reshape.6) | data formatting | bytes 524288 | tf_op jit(solution)/shard_map/reshape;reshape | solution.py:41
  53.0 0.7 convert_bitcast_fusion
  53.7 2.5 copy.48
  56.2 15.6 %all-to-all-done.3 = bf16[2,64,2,1024]{3,2,0,1:T(2,128)(2,1)S(1)} async-done(((bf16[2,64,2,1024]{3,2,0,1:T(2,128)(2,1)}), bf16[2,64,2,1024]{3,2,0,1:T(2,128)(2,1)S(1)}, u32[]{:S(2)}, u32[]{:S(2)}) %all-to-all-start.3) | async-done | bytes 524320 | tf_op jit(solution)/shard_map/all_to_all | solution.py:57
  71.8 5.5 all-to-all-start.1
  77.3 23.0 %all_gather.6 = bf16[2,512,128]{2,1,0:T(8,128)(2,1)S(1)} all-gather(bf16[2,32,128]{2,1,0:T(8,128)(2,1)S(1)} %copy-done.4), channel_id=1, replica_groups=mesh['dp'=16,'tensor'=32] {'dp'}, dimensions={1}, use_global_device_ids=true | all-gather | bytes 278528 | tf_op jit(solution)/shard_map/all_gather | solution.py:34
  100.3 0.9 copy.50
  101.2 1.2 copy.56
  102.4 1.2 all_to_all.55
  103.6 71.0 %all-to-all-done.1 = bf16[64,2,8,1024]{3,2,1,0:T(8,128)(2,1)S(1)} async-done(((bf16[64,2,8,1024]{3,2,1,0:T(8,128)(2,1)}), bf16[64,2,8,1024]{3,2,1,0:T(8,128)(2,1)S(1)}, u32[]{:S(2)}, u32[]{:S(2)}) %all-to-all-start.1) | async-done | bytes 2097184 | tf_op jit(solution)/shard_map/all_to_all | solution.py:46
  174.6 0.5 copy.49
  175.2 1.2 fusion.7
  176.3 1.5 fusion.14
  177.9 1.6 copy.58
  179.4 5.6 all-to-all-start.4
  185.1 0.5 fusion.19
  185.5 1.3 copy.52
  186.9 96.1 %all-to-all-done.4 = bf16[2,64,8,1024]{3,2,0,1:T(8,128)(2,1)} async-done(((bf16[2,64,8,1024]{3,2,0,1:T(8,128)(2,1)}), bf16[2,64,8,1024]{3,2,0,1:T(8,128)(2,1)}, u32[]{:S(2)}, u32[]{:S(2)}) %all-to-all-start.4) | async-done | bytes 2097184 | tf_op jit(solution)/shard_map/all_to_all | solution.py:70
  283.0 5.4 all-to-all-start.2
  288.4 0.0 all-reduce.3.cloned.1.call-start
  288.5 22.9 %all_gather.7 = bf16[2,128,512]{2,0,1:T(2,128)(2,1)S(1)} all-gather(bf16[2,8,512]{2,0,1:T(2,128)(2,1)S(1)} %copy.60), channel_id=1, replica_groups=mesh['dp'=16,'tensor'=32] {'dp'}, dimensions={1}, use_global_device_ids=true | all-gather | bytes 278528 | tf_op jit(solution)/shard_map/all_gather | solution.py:88
  311.4 0.9 copy.61
  312.3 1.3 dynamic-slice
  314.3 1.9 fusion.26
  316.1 0.3 copy.65
  316.4 1.0 copy.66
  317.5 0.0 all-reduce.3.cloned.1.call-update
  317.5 0.0 reduce-scatter.4.cloned.1.call-start
  317.5 5.1 copy.84
  322.6 2.7 all_to_all.59
  325.4 0.7 fusion.25
  326.1 0.2 copy.63
  326.3 0.8 copy.76
  327.1 141.6 %all-reduce.3.cloned.1.call-done = bf16[512,2,128]{2,1,0:T(2,128)(2,1)} async-done(((bf16[512,2,128]{2,1,0:T(2,128)(2,1)}), bf16[512,2,128]{2,1,0:T(2,128)(2,1)}) %all-reduce.3.cloned.1.call-update) | async-done | bytes 262160
  468.7 0.7 convert_bitcast_fusion.1
  469.4 0.6 copy.67
  470.1 1.2 copy.53
  471.2 2.0 reshape_reshape.7
  473.3 2.2 fusion.15
  475.5 87.8 %reduce-scatter.4.cloned.1.call-done = bf16[8,1024]{1,0:T(8,128)(2,1)} async-done(((bf16[128,1024]{1,0:T(8,128)(2,1)}), bf16[8,1024]{1,0:T(8,128)(2,1)}) %reduce-scatter.4.cloned.1.call-update) | async-done | bytes 16400
  563.3 1.3 convert_bitcast_fusion.2
  (14 shorter events, 0.1 us)
Async XLA Ops:
  7.2 45.8 %copy-start = (bf16[256,1024]{1,0:T(8,128)(2,1)S(1)}, bf16[256,1024]{1,0:T(8,128)(2,1)}, u32[]{:S(2)}) copy-start(bf16[256,1024]{1,0:T(8,128)(2,1)} %param.4) | copy-start | bytes 1572868
  8.7 16.6 %all-to-all-start = ((bf16[16,2,8,512]{3,2,1,0:T(8,128)(2,1)}), bf16[16,2,8,512]{3,2,1,0:T(8,128)(2,1)S(1)}, u32[]{:S(2)}, u32[]{:S(2)}) async-start(bf16[16,2,8,512]{3,2,1,0:T(8,128)(2,1)} %stack.2), calls=%async_computation | async-start | bytes 524288 | tf_op jit(solution)/shard_map/all_to_all | solution.py:15
  25.3 46.5 %all-to-all-start.3 = ((bf16[2,64,2,1024]{3,2,0,1:T(2,128)(2,1)}), bf16[2,64,2,1024]{3,2,0,1:T(2,128)(2,1)S(1)}, u32[]{:S(2)}, u32[]{:S(2)}) async-start(bf16[2,64,2,1024]{3,2,0,1:T(2,128)(2,1)} %copy.54), calls=%async_computation.3 | async-start | bytes 1048576 | tf_op jit(solution)/shard_map/all_to_all | solution.py:57
  53.7 23.6 %copy-start.4 = (bf16[2,32,128]{2,1,0:T(8,128)(2,1)S(1)}, bf16[2,32,128]{2,1,0:T(8,128)(2,1)}, u32[]{:S(2)}) copy-start(bf16[2,32,128]{2,1,0:T(8,128)(2,1)} %param.6) | copy-start | bytes 49156
  71.8 102.9 %all-to-all-start.1 = ((bf16[64,2,8,1024]{3,2,1,0:T(8,128)(2,1)}), bf16[64,2,8,1024]{3,2,1,0:T(8,128)(2,1)S(1)}, u32[]{:S(2)}, u32[]{:S(2)}) async-start(bf16[64,2,8,1024]{3,2,1,0:T(8,128)(2,1)} %copy.48), calls=%async_computation.1 | async-start | bytes 4194304 | tf_op jit(solution)/shard_map/all_to_all | solution.py:46
  103.6 72.7 %copy-start.1 = (bf16[64,2,2,1024]{3,0,2,1:T(8,128)(2,1)}, bf16[64,2,2,1024]{3,0,2,1:T(8,128)(2,1)S(1)}, u32[]{:S(2)}) copy-start(bf16[64,2,2,1024]{3,0,2,1:T(8,128)(2,1)S(1)} %all_to_all.55) | copy-start | bytes 1572868
  175.1 1.2 copy-start.2
  179.4 109.1 %copy-start.3 = (bf16[2,8,512]{2,1,0:T(8,128)(2,1)S(1)}, bf16[2,8,512]{2,1,0:T(8,128)(2,1)}, u32[]{:S(2)}) copy-start(bf16[2,8,512]{2,1,0:T(8,128)(2,1)} %param.5) | copy-start | bytes 49156
  179.4 103.6 %all-to-all-start.4 = ((bf16[2,64,8,1024]{3,2,0,1:T(8,128)(2,1)}), bf16[2,64,8,1024]{3,2,0,1:T(8,128)(2,1)}, u32[]{:S(2)}, u32[]{:S(2)}) async-start(bf16[2,64,8,1024]{3,2,0,1:T(8,128)(2,1)} %copy.58), calls=%async_computation.4 | async-start | bytes 4194304 | tf_op jit(solution)/shard_map/all_to_all | solution.py:70
  283.0 187.1 %all-to-all-start.2 = ((bf16[64,2,2,1024]{3,2,1,0:T(2,128)(2,1)}), bf16[64,2,2,1024]{3,2,1,0:T(2,128)(2,1)S(1)}, u32[]{:S(2)}, u32[]{:S(2)}) async-start(bf16[64,2,2,1024]{3,2,1,0:T(2,128)(2,1)} %copy.52), calls=%async_computation.2 | async-start | bytes 1048576 | tf_op jit(solution)/shard_map/all_to_all | solution.py:53
  288.4 180.3 %all-reduce.3.cloned.1.call-start = ((), (), s32[]{:S(2)}) async-start(), calls=%async_computation.7 | async-start | bytes 524288
  317.5 245.8 %reduce-scatter.4.cloned.1.call-start = ((), (), s32[]{:S(2)}) async-start(), calls=%async_computation.6 | async-start | bytes 278528
Sparse Core Ops, SparseCore 0:
  317.6 151.0 all-reduce.2
  473.9 89.3 reduce-scatter.3
